TPU v7x, 32 devices: a whole 2x2x4 slice. The times are simulated.
32 devices in a mesh: videos: 2 (over y), rows: 4 (over z), cols: 4 (over x, core).
Axes of the slice: x: 2, y: 2, z: 4, core: 2. Of those that a mesh axis runs over, the one named last changes fastest.
Arguments:
- hidden: bfloat16 [2, 16, 128, 384], P('videos', 'rows', 'cols'), parts along dimension 0, may hold values from -40 to 40
- frame_cache: bfloat16 [2, 2, 16, 128, 384], P('videos', None, 'rows', 'cols'), parts along dimension 0, may hold values from -6 to 6
- shortcut: bfloat16 [2, 16, 128, 384], P('videos', 'rows', 'cols'), parts along dimension 0, may hold values from -40 to 40
- gain_one: float32 [384], replicated, may hold values from 0.5 to 1.5
- conv_weight: bfloat16 [3, 3, 3, 384, 384], replicated, may hold values from -0.0625 to 0.0625
- conv_bias: float32 [384], replicated, may hold values from -2 to 2
- gain_two: float32 [384], replicated, may hold values from 0.5 to 1.5
- query_weight: bfloat16 [384, 384], replicated, may hold values from -1 to 1
- query_bias: float32 [384], replicated, may hold values from -3 to 3
- key_weight: bfloat16 [384, 384], replicated, may hold values from -1 to 1
- value_weight: bfloat16 [384, 384], replicated, may hold values from -0.3125 to 0.3125
- value_bias: float32 [384], replicated, may hold values from -3 to 3
- out_weight: bfloat16 [384, 384], replicated, may hold values from -0.3125 to 0.3125
- out_bias: float32 [384], replicated, may hold values from -2 to 2
Outputs:
- decoded: bfloat16 [2, 16, 128, 384], P('videos', 'rows', 'cols'), parts along dimension 0
There are 2 independent parts, one for each index of `videos`. A program takes and returns all parts, laid end to end along the dimension named above; an argument that names none is the same for every part. Nothing has to cross between parts.
All inputs are finite; a program needn't handle non-finite values.
Results may differ from a plain program's by a relative error of at most 0.0065.
Values may be sent and summed in bfloat16 or wider, within the bound.
No kernel may reach another device: no remote copies, remote signals or barrier semaphores. Data moves between devices by JAX's collectives and lax.ppermute only.
A program may use at most 128 MiB of HBM per device.

v0:
```python
import jax
import jax.numpy as jnp
from jax import lax
from jax.sharding import PartitionSpec as P

norm_epsilon = 1e-06


def padded(cells, sides, width):
    for axis, dim in sides:
        count = lax.axis_size(axis)
        ends = count - 1
        head = lax.slice_in_dim(cells, 0, width, axis=dim)
        tail = lax.slice_in_dim(cells, cells.shape[dim] - width, cells.shape[dim], axis=dim)
        cells = jnp.concatenate(
            [
                lax.ppermute(tail, axis, [(i, (i + 1) % count) for i in range(ends)]),
                cells,
                lax.ppermute(head, axis, [((i + 1) % count, i) for i in range(ends)]),
            ],
            axis=dim,
        )
    return cells


def normalize(field_rows, gain):
    mean_square = jnp.mean(field_rows * field_rows, axis=1, keepdims=True)
    return field_rows * lax.rsqrt(mean_square + norm_epsilon) * gain


def per_device(
    hidden,
    frame_cache,
    shortcut,
    gain_one,
    conv_weight,
    conv_bias,
    gain_two,
    query_weight,
    query_bias,
    key_weight,
    value_weight,
    value_bias,
    out_weight,
    out_bias,
):
    tile_rows = hidden.shape[1]
    tile_cols = hidden.shape[2]
    channels = hidden.shape[3]
    current = hidden[0].reshape(tile_rows * tile_cols, channels).astype(jnp.float32)
    activated = jax.nn.silu(normalize(current, gain_one)).astype(jnp.bfloat16)
    stacked = jnp.concatenate(
        [frame_cache[0], activated.reshape(1, tile_rows, tile_cols, channels)], axis=0
    )
    rimmed = padded(stacked, (("rows", 1), ("cols", 2)), 1)
    convolved = (
        lax.conv_general_dilated(
            rimmed[None],
            conv_weight,
            (1, 1, 1),
            "VALID",
            dimension_numbers=("NDHWC", "DHWIO", "NDHWC"),
            preferred_element_type=jnp.float32,
        )[0, 0]
        + conv_bias
    )
    mixed = (
        (shortcut[0].astype(jnp.float32) + convolved)
        .astype(jnp.bfloat16)
        .reshape(tile_rows * tile_cols, channels)
    )
    normed = normalize(mixed.astype(jnp.float32), gain_two).astype(jnp.bfloat16)
    queries = (
        jnp.dot(normed, query_weight, preferred_element_type=jnp.float32) + query_bias
    ).astype(jnp.bfloat16)
    score_scale = float(channels) ** (-0.5)
    query_count = queries.shape[0]
    piece = lax.all_gather(normed, ("rows", "cols"), axis=0, tiled=True)
    key_rows = jnp.dot(piece, key_weight, preferred_element_type=jnp.float32).astype(jnp.bfloat16)
    value_rows = (
        jnp.dot(piece, value_weight, preferred_element_type=jnp.float32) + value_bias
    ).astype(jnp.bfloat16)
    running_max = jnp.full((query_count,), -1e30, jnp.float32)
    scores = (
        jnp.einsum("qc,kc->qk", queries, key_rows, preferred_element_type=jnp.float32) * score_scale
    )
    new_max = jnp.maximum(running_max, jnp.max(scores, axis=1))
    expos = jnp.exp(scores - new_max[:, None])
    new_sum = jnp.sum(expos, axis=1)
    new_weighted = jnp.dot(
        expos.astype(jnp.bfloat16), value_rows, preferred_element_type=jnp.float32
    )
    attended = (new_weighted / new_sum[:, None]).astype(jnp.bfloat16)
    projected = jnp.dot(attended, out_weight, preferred_element_type=jnp.float32) + out_bias
    decoded = (mixed.astype(jnp.float32) + projected).astype(jnp.bfloat16)
    return decoded.reshape(1, tile_rows, tile_cols, channels)


def solution(mesh):
    placed = (
        P("videos", "rows", "cols", None),
        P("videos", None, "rows", "cols", None),
        P("videos", "rows", "cols", None),
        P(),
        P(),
        P(),
        P(),
        P(),
        P(),
        P(),
        P(),
        P(),
        P(),
        P(),
    )
    return jax.shard_map(
        per_device,
        mesh=mesh,
        in_specs=placed,
        out_specs=P("videos", "rows", "cols", None),
        check_vma=False,
    )
```

profile of v0, /device:TPU:0, one launch (start us, length us, event | category | flops | bytes accessed | tf_op | source)
XLA Modules:
  0.0 91.4 jit_solution(13943314025765096930)
XLA Ops:
  6.5 0.0 copy-start
  6.5 0.0 all-gather.2.cloned.1.call-start
  6.5 1.0 %fusion.18 = f32[4,32]{1,0:T(4,128)S(1)} fusion(bf16[1,4,32,384]{3,2,1,0:T(8,128)(2,1)} %param.14), kind=kLoop, calls=%fused_computation.28 | loop fusion | flops 147328 | bytes 98816 | tf_op jit(solution)/shard_map/reduce_sum | solution.py:27
  7.6 1.0 %fusion.25 = bf16[1,4,32,384]{3,2,1,0:T(8,128)(2,1)S(1)} fusion(bf16[1,4,32,384]{3,2,1,0:T(8,128)(2,1)} %param.14, f32[384]{0:T(512)} %param.17, f32[4,32]{1,0:T(4,128)S(1)} %add_rsqrt_fusion.1), kind=kLoop, calls=%fused_computation.35 | loop fusion | flops 393216 | bytes 198656 | tf_op jit(solution)/shard_map/convert_element_type | solution.py:51
  8.6 0.9 pad_maximum_fusion.1
  9.5 5.0 %collective-permute-start = (bf16[3,1,32,384]{3,2,1,0:T(8,128)(2,1)S(1)}, bf16[3,1,32,384]{3,2,1,0:T(8,128)(2,1)S(1)}, u32[]{:S(2)}, u32[]{:S(2)}) collective-permute-start(bf16[3,1,32,384]{3,2,1,0:T(8,128)(2,1)S(1)} %get-tuple-element.9), channel_id=1, source_target_pairs={{0,4},{4,8},{8,12},{1,5},{5,9},{9,13},{2,6},{6,10},{10,14},{3,7},{... | collective-permute-start | bytes 221192 | tf_op jit(solution)/shard_map/ppermute | solution.py:17
  14.4 1.3 %collective-permute-start.1 = (bf16[3,1,32,384]{3,2,1,0:T(8,128)(2,1)S(1)}, bf16[3,1,32,384]{3,2,1,0:T(8,128)(2,1)S(1)}, u32[]{:S(2)}, u32[]{:S(2)}) collective-permute-start(bf16[3,1,32,384]{3,2,1,0:T(8,128)(2,1)S(1)} %get-tuple-element.10), channel_id=1, source_target_pairs={{4,0},{8,4},{12,8},{5,1},{9,5},{13,9},{6,2},{10,6},{14,10},{7,3},{... | collective-permute-start | bytes 221192 | tf_op jit(solution)/shard_map/ppermute | solution.py:19
  15.7 0.7 collective-permute-done
  16.4 4.3 %collective-permute-done.1 = bf16[3,1,32,384]{3,2,1,0:T(8,128)(2,1)S(1)} collective-permute-done((bf16[3,1,32,384]{3,2,1,0:T(8,128)(2,1)S(1)}, bf16[3,1,32,384]{3,2,1,0:T(8,128)(2,1)S(1)}, u32[]{:S(2)}, u32[]{:S(2)}) %collective-permute-start.1) | collective-permute-done | bytes 73760 | tf_op jit(solution)/shard_map/ppermute | solution.py:19
  20.7 0.9 pad_maximum_fusion.5
  21.6 1.3 %collective-permute-start.2 = (bf16[3,6,1,384]{3,2,1,0:T(2,128)(2,1)S(1)}, bf16[3,6,1,384]{3,2,1,0:T(2,128)(2,1)S(1)}, u32[]{:S(2)}, u32[]{:S(2)}) collective-permute-start(bf16[3,6,1,384]{3,2,1,0:T(2,128)(2,1)S(1)} %get-tuple-element.7), channel_id=1, source_target_pairs={{0,1},{1,2},{2,3},{4,5},{5,6},{6,7},{8,9},{9,10},{10,11},{12,13},{... | collective-permute-start | bytes 41480 | tf_op jit(solution)/shard_map/ppermute | solution.py:17
  22.9 1.3 %collective-permute-start.3 = (bf16[3,6,1,384]{3,2,1,0:T(2,128)(2,1)S(1)}, bf16[3,6,1,384]{3,2,1,0:T(2,128)(2,1)S(1)}, u32[]{:S(2)}, u32[]{:S(2)}) collective-permute-start(bf16[3,6,1,384]{3,2,1,0:T(2,128)(2,1)S(1)} %get-tuple-element.8), channel_id=1, source_target_pairs={{1,0},{2,1},{3,2},{5,4},{6,5},{7,6},{9,8},{10,9},{11,10},{13,12},{... | collective-permute-start | bytes 41480 | tf_op jit(solution)/shard_map/ppermute | solution.py:19
  24.2 0.0 collective-permute-done.2
  24.2 3.5 %collective-permute-done.3 = bf16[3,6,1,384]{3,2,1,0:T(2,128)(2,1)S(1)} collective-permute-done((bf16[3,6,1,384]{3,2,1,0:T(2,128)(2,1)S(1)}, bf16[3,6,1,384]{3,2,1,0:T(2,128)(2,1)S(1)}, u32[]{:S(2)}, u32[]{:S(2)}) %collective-permute-start.3) | collective-permute-done | bytes 13856 | tf_op jit(solution)/shard_map/ppermute | solution.py:19
  27.7 1.2 %maximum_bitcast_fusion = bf16[3,6,1,34,384]{4,3,1,0,2:T(8,128)(2,1)S(1)} fusion(bf16[3,6,1,384]{3,2,1,0:T(2,128)(2,1)S(1)} %collective-permute-done.3, bf16[3,1,32,384]{3,2,1,0:T(8,128)(2,1)S(1)} %collective-permute-done.1, bf16[1,4,32,384]{3,2,1,0:T(8,128)(2,1)S(1)} %fusion.25, bf16[2,4,32,384]{3,2,1,0:T(8,128)(2,1)} %bitcast.40, ...), kind=kLoop, calls=%fused_computation.22 | loop fusion | flops 2820096 | bytes 940032 | tf_op jit(solution)/shard_map/broadcast_in_dim | solution.py:58
  28.9 0.1 copy.48
  29.0 0.0 copy-start.10
  29.0 0.1 pad.clone
  29.1 0.1 copy.41
  29.2 0.1 slice.18
  29.3 0.4 copy-done.10
  29.7 5.2 %convolution_select_fusion = f32[1,4,8,5,384]{4,2,3,1,0:T(8,128)S(1)} fusion(bf16[3,3,3,384,384]{4,3,2,1,0:T(8,128)(2,1)} %param.18, bf16[3,6,1,7,2,384]{5,3,4,1,0,2:T(8,128)(2,1)S(1)} %slice.18, bf16[3,6,1,8,5,384]{5,3,4,1,0,2:T(8,128)(2,1)S(1)} %copy.41, pred[8,5]{0,1:T(8,128)(4,1)S(1)} %copy-done.10), kind=kOutput, calls=%fused_computation.9 | convolution fusion | flops 1276403712 | bytes 8954920 | tf_op jit(solution)/shard_map/conv_general_dilated | solution.py:57
  34.9 0.0 copy-start.5
  34.9 0.0 copy-start.3
  34.9 0.0 copy-start.6
  34.9 0.1 copy.42
  35.0 0.0 copy-done.1
  35.0 0.0 copy-done.4
  35.1 0.1 multiply_reduce_fusion
  35.2 0.1 rsqrt.21
  35.3 0.3 copy-done.5
  35.6 0.7 fusion.27
  36.3 0.0 all-gather.2.cloned.1.call-update
  36.3 0.0 copy-done.3
  36.3 0.0 copy-done.6
  36.3 1.1 %fusion.3 = bf16[128,384]{1,0:T(8,128)(2,1)S(1)} fusion(bf16[128,384]{1,0:T(8,128)(2,1)} %get-tuple-element.5, bf16[384,384]{1,0:T(8,128)(2,1)S(1)} %copy-done.3, f32[384]{0:T(512)S(1)} %copy-done.6), kind=kOutput, calls=%fused_computation.10 | convolution fusion | flops 37847040 | bytes 493056 | tf_op jit(solution)/shard_map/dot_general | solution.py:74
  37.4 0.0 copy-start.9
  37.5 40.1 %all-gather.2.cloned.1.call-done = bf16[2048,384]{1,0:T(8,128)(2,1)} async-done(((bf16[128,384]{1,0:T(8,128)(2,1)}), bf16[2048,384]{1,0:T(8,128)(2,1)}) %all-gather.2.cloned.1.call-update) | async-done | bytes 1572880 | tf_op jit(solution)/shard_map/all_gather | solution.py:78
  77.6 0.0 copy-done
  77.6 3.1 %fusion.36 = (f32[128]{0:T(128)S(1)}, f32[128,2048]{1,0:T(8,128)S(1)}) fusion(bf16[128,384]{1,0:T(8,128)(2,1)S(1)} %fusion.3, bf16[2048,384]{1,0:T(8,128)(2,1)} %all-gather.2.cloned.1.call-done, bf16[384,384]{1,0:T(8,128)(2,1)S(1)} %copy-done), kind=kOutput, calls=%fused_computation.57 | convolution fusion | flops 806616960 | bytes 3015168 | tf_op jit(solution)/shard_map/qc,kc->qk/dot_general | solution.py:85
  80.7 0.3 fusion.7
  81.1 0.0 copy-done.8
  81.1 0.0 copy-start.2
  81.1 0.0 copy-start.7
  81.1 2.6 %fusion.6 = bf16[128,384]{1,0:T(8,128)(2,1)S(1)} fusion(bf16[2048,384]{1,0:T(8,128)(2,1)S(1)} %copy-done.8, bf16[384,384]{1,0:T(8,128)(2,1)} %param.24, f32[384]{0:T(512)S(1)} %copy-done.9, f32[128,2048]{1,0:T(8,128)S(1)} %get-tuple-element.12, f32[128]{0:T(128)S(1)} %broadcast_maximum_fusion, f32[128]{0:T(128)S(1)} %fusion.7), kind=kOutput, calls=%fused_computation.13 | convolution fusion | flops 807501824 | bytes 3017216 | tf_op jit(solution)/shard_map/dot_general | solution.py:90
  83.7 0.0 copy-done.2
  83.7 0.0 copy-done.7
  83.7 0.9 fusion.4
  (9 shorter events, 0.1 us)
Async XLA Ops:
  6.5 71.1 %copy-start = (bf16[384,384]{1,0:T(8,128)(2,1)S(1)}, bf16[384,384]{1,0:T(8,128)(2,1)}, u32[]{:S(2)}) copy-start(bf16[384,384]{1,0:T(8,128)(2,1)} %param.23) | copy-start | bytes 884740
  6.5 71.1 %all-gather.2.cloned.1.call-start = ((), (), s32[]{:S(2)}) async-start(), calls=%async_computation | async-start | bytes 1671168 | tf_op jit(solution)/shard_map/all_gather | solution.py:78
  9.5 6.9 %collective-permute-start = (bf16[3,1,32,384]{3,2,1,0:T(8,128)(2,1)S(1)}, bf16[3,1,32,384]{3,2,1,0:T(8,128)(2,1)S(1)}, u32[]{:S(2)}, u32[]{:S(2)}) collective-permute-start(bf16[3,1,32,384]{3,2,1,0:T(8,128)(2,1)S(1)} %get-tuple-element.9), channel_id=1, source_target_pairs={{0,4},{4,8},{8,12},{1,5},{5,9},{9,13},{2,6},{6,10},{10,14},{3,7},{... | collective-permute-start | bytes 221192 | tf_op jit(solution)/shard_map/ppermute | solution.py:17
  14.4 6.2 %collective-permute-start.1 = (bf16[3,1,32,384]{3,2,1,0:T(8,128)(2,1)S(1)}, bf16[3,1,32,384]{3,2,1,0:T(8,128)(2,1)S(1)}, u32[]{:S(2)}, u32[]{:S(2)}) collective-permute-start(bf16[3,1,32,384]{3,2,1,0:T(8,128)(2,1)S(1)} %get-tuple-element.10), channel_id=1, source_target_pairs={{4,0},{8,4},{12,8},{5,1},{9,5},{13,9},{6,2},{10,6},{14,10},{7,3},{... | collective-permute-start | bytes 221192 | tf_op jit(solution)/shard_map/ppermute | solution.py:19
  21.6 2.6 %collective-permute-start.2 = (bf16[3,6,1,384]{3,2,1,0:T(2,128)(2,1)S(1)}, bf16[3,6,1,384]{3,2,1,0:T(2,128)(2,1)S(1)}, u32[]{:S(2)}, u32[]{:S(2)}) collective-permute-start(bf16[3,6,1,384]{3,2,1,0:T(2,128)(2,1)S(1)} %get-tuple-element.7), channel_id=1, source_target_pairs={{0,1},{1,2},{2,3},{4,5},{5,6},{6,7},{8,9},{9,10},{10,11},{12,13},{... | collective-permute-start | bytes 41480 | tf_op jit(solution)/shard_map/ppermute | solution.py:17
  22.9 4.8 %collective-permute-start.3 = (bf16[3,6,1,384]{3,2,1,0:T(2,128)(2,1)S(1)}, bf16[3,6,1,384]{3,2,1,0:T(2,128)(2,1)S(1)}, u32[]{:S(2)}, u32[]{:S(2)}) collective-permute-start(bf16[3,6,1,384]{3,2,1,0:T(2,128)(2,1)S(1)} %get-tuple-element.8), channel_id=1, source_target_pairs={{1,0},{2,1},{3,2},{5,4},{6,5},{7,6},{9,8},{10,9},{11,10},{13,12},{... | collective-permute-start | bytes 41480 | tf_op jit(solution)/shard_map/ppermute | solution.py:19
  29.0 0.7 copy-start.10
  29.7 5.4 %copy-start.1 = (bf16[1,4,32,384]{3,2,1,0:T(8,128)(2,1)S(1)}, bf16[1,4,32,384]{3,2,1,0:T(8,128)(2,1)}, u32[]{:S(2)}) copy-start(bf16[1,4,32,384]{3,2,1,0:T(8,128)(2,1)} %param.16) | copy-start | bytes 294916
  29.7 5.4 %copy-start.4 = (f32[384]{0:T(512)S(1)}, f32[384]{0:T(512)}, u32[]{:S(2)}) copy-start(f32[384]{0:T(512)} %param.19) | copy-start | bytes 4612
  34.9 0.7 copy-start.5
  34.9 1.4 %copy-start.3 = (bf16[384,384]{1,0:T(8,128)(2,1)S(1)}, bf16[384,384]{1,0:T(8,128)(2,1)}, u32[]{:S(2)}) copy-start(bf16[384,384]{1,0:T(8,128)(2,1)} %param.21) | copy-start | bytes 884740
  34.9 1.4 %copy-start.6 = (f32[384]{0:T(512)S(1)}, f32[384]{0:T(512)}, u32[]{:S(2)}) copy-start(f32[384]{0:T(512)} %param.22) | copy-start | bytes 4612
  37.4 43.6 %copy-start.9 = (f32[384]{0:T(512)S(1)}, f32[384]{0:T(512)}, u32[]{:S(2)}) copy-start(f32[384]{0:T(512)} %param.25) | copy-start | bytes 4612
  77.6 3.5 %copy-start.8 = (bf16[2048,384]{1,0:T(8,128)(2,1)S(1)}, bf16[2048,384]{1,0:T(8,128)(2,1)}, u32[]{:S(2)}) copy-start(bf16[2048,384]{1,0:T(8,128)(2,1)} %all-gather.2.cloned.1.call-done) | copy-start | bytes 4718596
  81.1 2.6 %copy-start.2 = (bf16[384,384]{1,0:T(8,128)(2,1)S(1)}, bf16[384,384]{1,0:T(8,128)(2,1)}, u32[]{:S(2)}) copy-start(bf16[384,384]{1,0:T(8,128)(2,1)} %param.26) | copy-start | bytes 884740
  81.1 2.6 %copy-start.7 = (f32[384]{0:T(512)S(1)}, f32[384]{0:T(512)}, u32[]{:S(2)}) copy-start(f32[384]{0:T(512)} %param.27) | copy-start | bytes 4612
Sparse Core Ops, SparseCore 0:
  36.4 41.1 all-gather.1
where the time goes:
time: 91.8 us; the launch traced here: 91.4 us
  waiting for transfers between devices  48.6 us (53%)
  between operations  13.7 us (15%)
  matrix products  12.9 us (14%)
  starting transfers between devices  8.84 us (10%)
  other arithmetic  6.13 us (7%)
  local copies, waits for them, and re-layouts  1.27 us (1%)
    all_gather x1, waiting for transfers between devices, per_device(): piece = lax.all_gather(normed, ('rows', 'cols'), axis=0, tiled=True)  40.1 us
    ppermute x2, waiting for transfers between devices, padded(): lax.ppermute(head, axis, [((i + 1) % count, i) for i in range(ends)])  7.79 us
    ppermute x2, starting transfers between devices, padded(): lax.ppermute(tail, axis, [(i, (i + 1) % count) for i in range(ends)])  6.25 us
    conv_general_dilated x1, matrix products, per_device(): lax.conv_general_dilated(rimmed[None], conv_weight, (1, 1, 1), 'VALID', d...  5.21 us
    dot_general x1, matrix products, per_device(): jnp.einsum('qc,kc->qk', queries, key_rows, preferred_element_type=jnp.flo...  3.13 us
    ppermute x2, starting transfers between devices, padded(): lax.ppermute(head, axis, [((i + 1) % count, i) for i in range(ends)])  2.58 us
    dot_general x1, matrix products, per_device(): jnp.dot(expos.astype(jnp.bfloat16), value_rows, preferred_element_type=jn...  2.56 us
  transfers between devices with their start and end apart: 5, of which 4 were waited for; matrix products, arithmetic and copies ran while one was open for 1% of the time, Pallas kernels for 0%

commit v1 on v0

--- a/solution.py
+++ b/solution.py
@@ -75,7 +75,29 @@
     ).astype(jnp.bfloat16)
     score_scale = float(channels) ** (-0.5)
     query_count = queries.shape[0]
-    piece = lax.all_gather(normed, ("rows", "cols"), axis=0, tiled=True)
+    ways, here, step = (
+        lax.axis_size(("rows", "cols")),
+        lax.axis_index(("rows", "cols")),
+        normed.shape[0],
+    )
+    shape = [n * ways if d == 0 else n for d, n in enumerate(normed.shape)]
+    full = lax.dynamic_update_slice_in_dim(
+        jnp.zeros(shape, normed.dtype), normed, here * step, axis=0
+    )
+    going_up = going_down = normed
+    for far in range(1, ways // 2 + 1):
+        going_up = lax.ppermute(
+            going_up, ("rows", "cols"), [(d, (d + 1) % ways) for d in range(ways)]
+        )
+        full = lax.dynamic_update_slice_in_dim(full, going_up, (here - far) % ways * step, axis=0)
+        if 2 * far < ways:
+            going_down = lax.ppermute(
+                going_down, ("rows", "cols"), [(d, (d - 1) % ways) for d in range(ways)]
+            )
+            full = lax.dynamic_update_slice_in_dim(
+                full, going_down, (here + far) % ways * step, axis=0
+            )
+    piece = full
     key_rows = jnp.dot(piece, key_weight, preferred_element_type=jnp.float32).astype(jnp.bfloat16)
     value_rows = (
         jnp.dot(piece, value_weight, preferred_element_type=jnp.float32) + value_bias

time: 91.8 us -> 86.2 us (0.939)
  starting transfers between devices: 8.84 us -> 44.3 us
  waiting for transfers between devices: 48.6 us -> 24.3 us
  between operations: 13.7 us -> 0.64 us
  matrix products: 12.9 us -> 10.4 us
  other arithmetic: 6.13 us -> 4.6 us
    all_gather x1 -> x0, waiting for transfers between devices: 40.1 us -> none  [per_device(): piece = lax.all_gather(normed, ('rows', 'cols'), axis=0, tiled=True)]
    ppermute x0 -> x15, starting transfers between devices: none -> 33.1 us  [the longest x7 31.3 us: per_device(): lax.ppermute(going_down, ('rows', 'cols'), [(d, (d - 1) % ways) for d in...]
    ppermute x0 -> x15, waiting for transfers between devices: none -> 21.8 us  [the longest x8 21.5 us: per_device(): lax.ppermute(going_up, ('rows', 'cols'), [(d, (d + 1) % ways) for d in ra...]
    ppermute x2, waiting for transfers between devices: 7.79 us -> 0.39 us  [padded(): lax.ppermute(head, axis, [((i + 1) % count, i) for i in range(ends)])]
    ppermute x2, starting transfers between devices: 6.25 us -> 8.62 us  [padded(): lax.ppermute(tail, axis, [(i, (i + 1) % count) for i in range(ends)])]
    dot_general x1, matrix products: 3.13 us -> 1.6 us  [per_device(): jnp.einsum('qc,kc->qk', queries, key_rows, preferred_element_type=jnp.flo...]
    ppermute x2, waiting for transfers between devices: 0.66 us -> 2.08 us  [padded(): lax.ppermute(tail, axis, [(i, (i + 1) % count) for i in range(ends)])]
    broadcast_in_dim x1, other arithmetic: 1.18 us -> 0.26 us  [per_device(): rimmed[None]]
  transfers between devices with their start and end apart: 5 -> 19, of which waited for: 4 -> 13; matrix products, arithmetic and copies ran while one was open for 1% -> 1% of each run, Pallas kernels for 0% -> 0%
where the time goes in v1:
time: 86.2 us; the launch traced here: 85.8 us
  starting transfers between devices  44.3 us (51%)
  waiting for transfers between devices  24.3 us (28%)
  matrix products  10.4 us (12%)
  other arithmetic  4.6 us (5%)
  local copies, waits for them, and re-layouts  1.58 us (2%)
    ppermute x7, starting transfers between devices, per_device(): lax.ppermute(going_down, ('rows', 'cols'), [(d, (d - 1) % ways) for d in...  31.3 us
    ppermute x8, waiting for transfers between devices, per_device(): lax.ppermute(going_up, ('rows', 'cols'), [(d, (d + 1) % ways) for d in ra...  21.5 us
    ppermute x2, starting transfers between devices, padded(): lax.ppermute(tail, axis, [(i, (i + 1) % count) for i in range(ends)])  8.62 us
    conv_general_dilated x1, matrix products, per_device(): lax.conv_general_dilated(rimmed[None], conv_weight, (1, 1, 1), 'VALID', d...  5.2 us
    ppermute x2, starting transfers between devices, padded(): lax.ppermute(head, axis, [((i + 1) % count, i) for i in range(ends)])  2.58 us
    dot_general x1, matrix products, per_device(): jnp.dot(expos.astype(jnp.bfloat16), value_rows, preferred_element_type=jn...  2.56 us
    ppermute x2, waiting for transfers between devices, padded(): lax.ppermute(tail, axis, [(i, (i + 1) % count) for i in range(ends)])  2.08 us
    ppermute x8, starting transfers between devices, per_device(): lax.ppermute(going_up, ('rows', 'cols'), [(d, (d + 1) % ways) for d in ra...  1.75 us
  transfers between devices with their start and end apart: 19, of which 13 were waited for; matrix products, arithmetic and copies ran while one was open for 1% of the time, Pallas kernels for 0%

profile of v1, /device:TPU:0, one launch (start us, length us, event | category | flops | bytes accessed | tf_op | source)
XLA Modules:
  0.0 85.8 jit_solution(5190045588896250300)
XLA Ops:
  0.0 1.0 %fusion.18 = f32[4,32]{1,0:T(4,128)S(1)} fusion(bf16[1,4,32,384]{3,2,1,0:T(8,128)(2,1)} %param.14), kind=kLoop, calls=%fused_computation.28 | loop fusion | flops 147328 | bytes 98816 | tf_op jit(solution)/shard_map/reduce_sum | solution.py:27
  1.1 1.0 %fusion.25 = bf16[1,4,32,384]{3,2,1,0:T(8,128)(2,1)S(1)} fusion(bf16[1,4,32,384]{3,2,1,0:T(8,128)(2,1)} %param.14, f32[384]{0:T(512)} %param.17, f32[4,32]{1,0:T(4,128)S(1)} %add_rsqrt_fusion.1), kind=kLoop, calls=%fused_computation.35 | loop fusion | flops 393216 | bytes 198656 | tf_op jit(solution)/shard_map/convert_element_type | solution.py:51
  2.1 0.9 pad_maximum_fusion.1
  3.0 1.3 %collective-permute-start.1 = (bf16[3,1,32,384]{3,2,1,0:T(8,128)(2,1)S(1)}, bf16[3,1,32,384]{3,2,1,0:T(8,128)(2,1)S(1)}, u32[]{:S(2)}, u32[]{:S(2)}) collective-permute-start(bf16[3,1,32,384]{3,2,1,0:T(8,128)(2,1)S(1)} %get-tuple-element.10), channel_id=1, source_target_pairs={{4,0},{8,4},{12,8},{5,1},{9,5},{13,9},{6,2},{10,6},{14,10},{7,3},{... | collective-permute-start | bytes 221192 | tf_op jit(solution)/shard_map/ppermute | solution.py:19
  4.3 5.6 %collective-permute-start = (bf16[3,1,32,384]{3,2,1,0:T(8,128)(2,1)S(1)}, bf16[3,1,32,384]{3,2,1,0:T(8,128)(2,1)S(1)}, u32[]{:S(2)}, u32[]{:S(2)}) collective-permute-start(bf16[3,1,32,384]{3,2,1,0:T(8,128)(2,1)S(1)} %get-tuple-element.9), channel_id=1, source_target_pairs={{0,4},{4,8},{8,12},{1,5},{5,9},{9,13},{2,6},{6,10},{10,14},{3,7},{... | collective-permute-start | bytes 221192 | tf_op jit(solution)/shard_map/ppermute | solution.py:17
  9.9 0.4 collective-permute-done.1
  10.2 1.6 %collective-permute-done = bf16[3,1,32,384]{3,2,1,0:T(8,128)(2,1)S(1)} collective-permute-done((bf16[3,1,32,384]{3,2,1,0:T(8,128)(2,1)S(1)}, bf16[3,1,32,384]{3,2,1,0:T(8,128)(2,1)S(1)}, u32[]{:S(2)}, u32[]{:S(2)}) %collective-permute-start) | collective-permute-done | bytes 73760 | tf_op jit(solution)/shard_map/ppermute | solution.py:17
  11.8 0.9 %pad_maximum_fusion.5 = (bf16[3,6,1,384]{3,2,1,0:T(2,128)(2,1)S(1)}, bf16[3,6,1,384]{3,2,1,0:T(2,128)(2,1)S(1)}) fusion(bf16[3,1,32,384]{3,2,1,0:T(8,128)(2,1)S(1)} %collective-permute-done.1, bf16[3,1,32,384]{3,2,1,0:T(8,128)(2,1)S(1)} %collective-permute-done, bf16[1,4,32,384]{3,2,1,0:T(8,128)(2,1)S(1)} %fusion.25, bf16[2,4,32,384]{3,2,1,0:T(8,128)(2,1)} %bitcast.37), kind=kLoop, calls=%fused_computation.50 | loop fusion | flops 110592 | bytes 470016 | tf_op jit(solution)/shard_map/slice | solution.py:14
  12.7 1.3 %collective-permute-start.3 = (bf16[3,6,1,384]{3,2,1,0:T(2,128)(2,1)S(1)}, bf16[3,6,1,384]{3,2,1,0:T(2,128)(2,1)S(1)}, u32[]{:S(2)}, u32[]{:S(2)}) collective-permute-start(bf16[3,6,1,384]{3,2,1,0:T(2,128)(2,1)S(1)} %get-tuple-element.8), channel_id=1, source_target_pairs={{1,0},{2,1},{3,2},{5,4},{6,5},{7,6},{9,8},{10,9},{11,10},{13,12},{... | collective-permute-start | bytes 41480 | tf_op jit(solution)/shard_map/ppermute | solution.py:19
  14.0 3.0 %collective-permute-start.2 = (bf16[3,6,1,384]{3,2,1,0:T(2,128)(2,1)S(1)}, bf16[3,6,1,384]{3,2,1,0:T(2,128)(2,1)S(1)}, u32[]{:S(2)}, u32[]{:S(2)}) collective-permute-start(bf16[3,6,1,384]{3,2,1,0:T(2,128)(2,1)S(1)} %get-tuple-element.7), channel_id=1, source_target_pairs={{0,1},{1,2},{2,3},{4,5},{5,6},{6,7},{8,9},{9,10},{10,11},{12,13},{... | collective-permute-start | bytes 41480 | tf_op jit(solution)/shard_map/ppermute | solution.py:17
  17.4 0.5 collective-permute-done.2
  17.9 0.3 maximum_bitcast_fusion
  18.1 0.1 copy.48
  18.2 0.1 pad.clone
  18.4 0.1 copy.41
  18.4 0.1 slice.18
  18.5 0.4 copy-done.10
  18.9 5.2 %convolution_select_fusion = f32[1,4,8,5,384]{4,2,3,1,0:T(8,128)S(1)} fusion(bf16[3,3,3,384,384]{4,3,2,1,0:T(8,128)(2,1)} %param.18, bf16[3,6,1,7,2,384]{5,3,4,1,0,2:T(8,128)(2,1)S(1)} %slice.18, bf16[3,6,1,8,5,384]{5,3,4,1,0,2:T(8,128)(2,1)S(1)} %copy.41, pred[8,5]{0,1:T(8,128)(4,1)S(1)} %copy-done.10), kind=kOutput, calls=%fused_computation.9 | convolution fusion | flops 1276403712 | bytes 8954920 | tf_op jit(solution)/shard_map/conv_general_dilated | solution.py:57
  24.1 0.1 copy.42
  24.3 0.1 multiply_reduce_fusion
  24.4 0.1 rsqrt.21
  24.5 0.1 broadcast_in_dim.7
  24.7 0.1 copy-done.6
  24.8 0.1 constant_dynamic-update-slice_fusion.15
  24.9 1.7 %collective-permute-start.4 = (bf16[128,384]{1,0:T(8,128)(2,1)S(1)}, bf16[128,384]{1,0:T(8,128)(2,1)S(1)}, u32[]{:S(2)}, u32[]{:S(2)}) collective-permute-start(bf16[128,384]{1,0:T(8,128)(2,1)S(1)} %get-tuple-element.6), channel_id=1, source_target_pairs={{0,1},{1,2},{2,3},{3,4},{4,5},{5,6},{6,7},{7,8},{8,9},{9,10},{10,1... | collective-permute-start | bytes 294920 | tf_op jit(solution)/shard_map/ppermute | solution.py:89
  26.6 4.1 %collective-permute-start.5 = (bf16[128,384]{1,0:T(8,128)(2,1)S(1)}, bf16[128,384]{1,0:T(8,128)(2,1)S(1)}, u32[]{:S(2)}, u32[]{:S(2)}) collective-permute-start(bf16[128,384]{1,0:T(8,128)(2,1)S(1)} %get-tuple-element.6), channel_id=1, source_target_pairs={{0,15},{1,0},{2,1},{3,2},{4,3},{5,4},{6,5},{7,6},{8,7},{9,8},{10,9... | collective-permute-start | bytes 294920 | tf_op jit(solution)/shard_map/ppermute | solution.py:94
  30.7 0.2 fusion.3
  31.0 2.1 %collective-permute-done.4 = bf16[128,384]{1,0:T(8,128)(2,1)S(1)} collective-permute-done((bf16[128,384]{1,0:T(8,128)(2,1)S(1)}, bf16[128,384]{1,0:T(8,128)(2,1)S(1)}, u32[]{:S(2)}, u32[]{:S(2)}) %collective-permute-start.4) | collective-permute-done | bytes 98336 | tf_op jit(solution)/shard_map/ppermute | solution.py:89
  33.1 4.4 %collective-permute-start.7 = (bf16[128,384]{1,0:T(8,128)(2,1)S(1)}, bf16[128,384]{1,0:T(8,128)(2,1)S(1)}, u32[]{:S(2)}, u32[]{:S(2)}) collective-permute-start(bf16[128,384]{1,0:T(8,128)(2,1)S(1)} %collective-permute-done.5), channel_id=1, source_target_pairs={{0,15},{1,0},{2,1},{3,2},{4,3},{5,4},{6,5},{7,6},{8,7},{9,8},{10,9... | collective-permute-start | bytes 294920 | tf_op jit(solution)/shard_map/ppermute | solution.py:94
  37.6 2.2 %collective-permute-done.6 = bf16[128,384]{1,0:T(8,128)(2,1)S(1)} collective-permute-done((bf16[128,384]{1,0:T(8,128)(2,1)S(1)}, bf16[128,384]{1,0:T(8,128)(2,1)S(1)}, u32[]{:S(2)}, u32[]{:S(2)}) %collective-permute-start.6) | collective-permute-done | bytes 98336 | tf_op jit(solution)/shard_map/ppermute | solution.py:89
  39.8 4.5 %collective-permute-start.9 = (bf16[128,384]{1,0:T(8,128)(2,1)S(1)}, bf16[128,384]{1,0:T(8,128)(2,1)S(1)}, u32[]{:S(2)}, u32[]{:S(2)}) collective-permute-start(bf16[128,384]{1,0:T(8,128)(2,1)S(1)} %collective-permute-done.7), channel_id=1, source_target_pairs={{0,15},{1,0},{2,1},{3,2},{4,3},{5,4},{6,5},{7,6},{8,7},{9,8},{10,9... | collective-permute-start | bytes 294920 | tf_op jit(solution)/shard_map/ppermute | solution.py:94
  44.4 2.2 %collective-permute-done.8 = bf16[128,384]{1,0:T(8,128)(2,1)S(1)} collective-permute-done((bf16[128,384]{1,0:T(8,128)(2,1)S(1)}, bf16[128,384]{1,0:T(8,128)(2,1)S(1)}, u32[]{:S(2)}, u32[]{:S(2)}) %collective-permute-start.8) | collective-permute-done | bytes 98336 | tf_op jit(solution)/shard_map/ppermute | solution.py:89
  46.7 4.4 %collective-permute-start.11 = (bf16[128,384]{1,0:T(8,128)(2,1)S(1)}, bf16[128,384]{1,0:T(8,128)(2,1)S(1)}, u32[]{:S(2)}, u32[]{:S(2)}) collective-permute-start(bf16[128,384]{1,0:T(8,128)(2,1)S(1)} %collective-permute-done.9), channel_id=1, source_target_pairs={{0,15},{1,0},{2,1},{3,2},{4,3},{5,4},{6,5},{7,6},{8,7},{9,8},{10,9... | collective-permute-start | bytes 294920 | tf_op jit(solution)/shard_map/ppermute | solution.py:94
  51.1 2.2 %collective-permute-done.10 = bf16[128,384]{1,0:T(8,128)(2,1)S(1)} collective-permute-done((bf16[128,384]{1,0:T(8,128)(2,1)S(1)}, bf16[128,384]{1,0:T(8,128)(2,1)S(1)}, u32[]{:S(2)}, u32[]{:S(2)}) %collective-permute-start.10) | collective-permute-done | bytes 98336 | tf_op jit(solution)/shard_map/ppermute | solution.py:89
  53.4 4.5 %collective-permute-start.13 = (bf16[128,384]{1,0:T(8,128)(2,1)S(1)}, bf16[128,384]{1,0:T(8,128)(2,1)S(1)}, u32[]{:S(2)}, u32[]{:S(2)}) collective-permute-start(bf16[128,384]{1,0:T(8,128)(2,1)S(1)} %collective-permute-done.11), channel_id=1, source_target_pairs={{0,15},{1,0},{2,1},{3,2},{4,3},{5,4},{6,5},{7,6},{8,7},{9,8},{10,9... | collective-permute-start | bytes 294920 | tf_op jit(solution)/shard_map/ppermute | solution.py:94
  58.0 2.1 %collective-permute-done.12 = bf16[128,384]{1,0:T(8,128)(2,1)S(1)} collective-permute-done((bf16[128,384]{1,0:T(8,128)(2,1)S(1)}, bf16[128,384]{1,0:T(8,128)(2,1)S(1)}, u32[]{:S(2)}, u32[]{:S(2)}) %collective-permute-start.12) | collective-permute-done | bytes 98336 | tf_op jit(solution)/shard_map/ppermute | solution.py:89
  60.1 0.0 collective-permute-done.13
  60.2 4.6 %collective-permute-start.15 = (bf16[128,384]{1,0:T(8,128)(2,1)S(1)}, bf16[128,384]{1,0:T(8,128)(2,1)S(1)}, u32[]{:S(2)}, u32[]{:S(2)}) collective-permute-start(bf16[128,384]{1,0:T(8,128)(2,1)S(1)} %collective-permute-done.13), channel_id=1, source_target_pairs={{0,15},{1,0},{2,1},{3,2},{4,3},{5,4},{6,5},{7,6},{8,7},{9,8},{10,9... | collective-permute-start | bytes 294920 | tf_op jit(solution)/shard_map/ppermute | solution.py:94
  64.8 2.1 %collective-permute-done.14 = bf16[128,384]{1,0:T(8,128)(2,1)S(1)} collective-permute-done((bf16[128,384]{1,0:T(8,128)(2,1)S(1)}, bf16[128,384]{1,0:T(8,128)(2,1)S(1)}, u32[]{:S(2)}, u32[]{:S(2)}) %collective-permute-start.14) | collective-permute-done | bytes 98336 | tf_op jit(solution)/shard_map/ppermute | solution.py:89
  66.9 0.1 collective-permute-done.15
  67.0 4.6 %collective-permute-start.17 = (bf16[128,384]{1,0:T(8,128)(2,1)S(1)}, bf16[128,384]{1,0:T(8,128)(2,1)S(1)}, u32[]{:S(2)}, u32[]{:S(2)}) collective-permute-start(bf16[128,384]{1,0:T(8,128)(2,1)S(1)} %collective-permute-done.15), channel_id=1, source_target_pairs={{0,15},{1,0},{2,1},{3,2},{4,3},{5,4},{6,5},{7,6},{8,7},{9,8},{10,9... | collective-permute-start | bytes 294920 | tf_op jit(solution)/shard_map/ppermute | solution.py:94
  71.7 2.0 %collective-permute-done.16 = bf16[128,384]{1,0:T(8,128)(2,1)S(1)} collective-permute-done((bf16[128,384]{1,0:T(8,128)(2,1)S(1)}, bf16[128,384]{1,0:T(8,128)(2,1)S(1)}, u32[]{:S(2)}, u32[]{:S(2)}) %collective-permute-start.16) | collective-permute-done | bytes 98336 | tf_op jit(solution)/shard_map/ppermute | solution.py:89
  73.6 0.2 collective-permute-done.17
  73.8 6.5 %collective-permute-done.18 = bf16[128,384]{1,0:T(8,128)(2,1)S(1)} collective-permute-done((bf16[128,384]{1,0:T(8,128)(2,1)S(1)}, bf16[128,384]{1,0:T(8,128)(2,1)S(1)}, u32[]{:S(2)}, u32[]{:S(2)}) %collective-permute-start.18) | collective-permute-done | bytes 98336 | tf_op jit(solution)/shard_map/ppermute | solution.py:89
  80.4 1.6 %fusion.36 = (f32[128]{0:T(128)S(1)}, f32[128,2048]{1,0:T(8,128)S(1)}) fusion(bf16[128,384]{1,0:T(8,128)(2,1)S(1)} %fusion.3, bf16[2048,384]{1,0:T(8,128)(2,1)S(1)} %constant_dynamic-update-slice_fusion, bf16[384,384]{1,0:T(8,128)(2,1)S(1)} %copy-done), kind=kOutput, calls=%fused_computation.73 | convolution fusion | flops 806616960 | bytes 3015168 | tf_op jit(solution)/shard_map/qc,kc->qk/dot_general | solution.py:107
  82.0 0.3 fusion.7
  82.4 2.6 %fusion.6 = bf16[128,384]{1,0:T(8,128)(2,1)S(1)} fusion(bf16[2048,384]{1,0:T(8,128)(2,1)S(1)} %constant_dynamic-update-slice_fusion, bf16[384,384]{1,0:T(8,128)(2,1)} %param.24, f32[384]{0:T(512)S(1)} %copy-done.9, f32[128,2048]{1,0:T(8,128)S(1)} %get-tuple-element.13, f32[128]{0:T(128)S(1)} %broadcast_maximum_fusion, f32[128]{0:T(128)S(1)} %fusion.7), kind=kOutput, calls=%fused_computation.13 | convolution fusion | flops 807501824 | bytes 3017216 | tf_op jit(solution)/shard_map/dot_general | solution.py:112
  84.9 0.9 fusion.4
  (52 shorter events, 0.5 us)
Async XLA Ops:
  0.0 80.4 %copy-start = (bf16[384,384]{1,0:T(8,128)(2,1)S(1)}, bf16[384,384]{1,0:T(8,128)(2,1)}, u32[]{:S(2)}) copy-start(bf16[384,384]{1,0:T(8,128)(2,1)} %param.23) | copy-start | bytes 884740
  0.0 17.9 %copy-start.1 = (bf16[1,2,4,32,384]{4,3,2,1,0:T(8,128)(2,1)S(1)}, bf16[1,2,4,32,384]{4,3,2,1,0:T(8,128)(2,1)}, u32[]{:S(2)}) copy-start(bf16[1,2,4,32,384]{4,3,2,1,0:T(8,128)(2,1)} %param.15) | copy-start | bytes 589828
  3.0 7.3 %collective-permute-start.1 = (bf16[3,1,32,384]{3,2,1,0:T(8,128)(2,1)S(1)}, bf16[3,1,32,384]{3,2,1,0:T(8,128)(2,1)S(1)}, u32[]{:S(2)}, u32[]{:S(2)}) collective-permute-start(bf16[3,1,32,384]{3,2,1,0:T(8,128)(2,1)S(1)} %get-tuple-element.10), channel_id=1, source_target_pairs={{4,0},{8,4},{12,8},{5,1},{9,5},{13,9},{6,2},{10,6},{14,10},{7,3},{... | collective-permute-start | bytes 221192 | tf_op jit(solution)/shard_map/ppermute | solution.py:19
  4.3 7.6 %collective-permute-start = (bf16[3,1,32,384]{3,2,1,0:T(8,128)(2,1)S(1)}, bf16[3,1,32,384]{3,2,1,0:T(8,128)(2,1)S(1)}, u32[]{:S(2)}, u32[]{:S(2)}) collective-permute-start(bf16[3,1,32,384]{3,2,1,0:T(8,128)(2,1)S(1)} %get-tuple-element.9), channel_id=1, source_target_pairs={{0,4},{4,8},{8,12},{1,5},{5,9},{9,13},{2,6},{6,10},{10,14},{3,7},{... | collective-permute-start | bytes 221192 | tf_op jit(solution)/shard_map/ppermute | solution.py:17
  12.7 4.7 %collective-permute-start.3 = (bf16[3,6,1,384]{3,2,1,0:T(2,128)(2,1)S(1)}, bf16[3,6,1,384]{3,2,1,0:T(2,128)(2,1)S(1)}, u32[]{:S(2)}, u32[]{:S(2)}) collective-permute-start(bf16[3,6,1,384]{3,2,1,0:T(2,128)(2,1)S(1)} %get-tuple-element.8), channel_id=1, source_target_pairs={{1,0},{2,1},{3,2},{5,4},{6,5},{7,6},{9,8},{10,9},{11,10},{13,12},{... | collective-permute-start | bytes 41480 | tf_op jit(solution)/shard_map/ppermute | solution.py:19
  14.0 3.9 %collective-permute-start.2 = (bf16[3,6,1,384]{3,2,1,0:T(2,128)(2,1)S(1)}, bf16[3,6,1,384]{3,2,1,0:T(2,128)(2,1)S(1)}, u32[]{:S(2)}, u32[]{:S(2)}) collective-permute-start(bf16[3,6,1,384]{3,2,1,0:T(2,128)(2,1)S(1)} %get-tuple-element.7), channel_id=1, source_target_pairs={{0,1},{1,2},{2,3},{4,5},{5,6},{6,7},{8,9},{9,10},{10,11},{12,13},{... | collective-permute-start | bytes 41480 | tf_op jit(solution)/shard_map/ppermute | solution.py:17
  18.2 0.7 copy-start.10
  18.9 5.4 %copy-start.2 = (bf16[1,4,32,384]{3,2,1,0:T(8,128)(2,1)S(1)}, bf16[1,4,32,384]{3,2,1,0:T(8,128)(2,1)}, u32[]{:S(2)}) copy-start(bf16[1,4,32,384]{3,2,1,0:T(8,128)(2,1)} %param.16) | copy-start | bytes 294916
  18.9 5.4 %copy-start.5 = (f32[384]{0:T(512)S(1)}, f32[384]{0:T(512)}, u32[]{:S(2)}) copy-start(f32[384]{0:T(512)} %param.19) | copy-start | bytes 4612
  24.1 0.7 copy-start.6
  24.2 6.5 %copy-start.4 = (bf16[384,384]{1,0:T(8,128)(2,1)S(1)}, bf16[384,384]{1,0:T(8,128)(2,1)}, u32[]{:S(2)}) copy-start(bf16[384,384]{1,0:T(8,128)(2,1)} %param.21) | copy-start | bytes 884740
  24.2 6.5 %copy-start.7 = (f32[384]{0:T(512)S(1)}, f32[384]{0:T(512)}, u32[]{:S(2)}) copy-start(f32[384]{0:T(512)} %param.22) | copy-start | bytes 4612
  24.9 8.2 %collective-permute-start.4 = (bf16[128,384]{1,0:T(8,128)(2,1)S(1)}, bf16[128,384]{1,0:T(8,128)(2,1)S(1)}, u32[]{:S(2)}, u32[]{:S(2)}) collective-permute-start(bf16[128,384]{1,0:T(8,128)(2,1)S(1)} %get-tuple-element.6), channel_id=1, source_target_pairs={{0,1},{1,2},{2,3},{3,4},{4,5},{5,6},{6,7},{7,8},{8,9},{9,10},{10,1... | collective-permute-start | bytes 294920 | tf_op jit(solution)/shard_map/ppermute | solution.py:89
  26.6 6.4 %collective-permute-start.5 = (bf16[128,384]{1,0:T(8,128)(2,1)S(1)}, bf16[128,384]{1,0:T(8,128)(2,1)S(1)}, u32[]{:S(2)}, u32[]{:S(2)}) collective-permute-start(bf16[128,384]{1,0:T(8,128)(2,1)S(1)} %get-tuple-element.6), channel_id=1, source_target_pairs={{0,15},{1,0},{2,1},{3,2},{4,3},{5,4},{6,5},{7,6},{8,7},{9,8},{10,9... | collective-permute-start | bytes 294920 | tf_op jit(solution)/shard_map/ppermute | solution.py:94
  33.1 6.7 %collective-permute-start.6 = (bf16[128,384]{1,0:T(8,128)(2,1)S(1)}, bf16[128,384]{1,0:T(8,128)(2,1)S(1)}, u32[]{:S(2)}, u32[]{:S(2)}) collective-permute-start(bf16[128,384]{1,0:T(8,128)(2,1)S(1)} %collective-permute-done.4), channel_id=1, source_target_pairs={{0,1},{1,2},{2,3},{3,4},{4,5},{5,6},{6,7},{7,8},{8,9},{9,10},{10,1... | collective-permute-start | bytes 294920 | tf_op jit(solution)/shard_map/ppermute | solution.py:89
  33.1 6.7 %collective-permute-start.7 = (bf16[128,384]{1,0:T(8,128)(2,1)S(1)}, bf16[128,384]{1,0:T(8,128)(2,1)S(1)}, u32[]{:S(2)}, u32[]{:S(2)}) collective-permute-start(bf16[128,384]{1,0:T(8,128)(2,1)S(1)} %collective-permute-done.5), channel_id=1, source_target_pairs={{0,15},{1,0},{2,1},{3,2},{4,3},{5,4},{6,5},{7,6},{8,7},{9,8},{10,9... | collective-permute-start | bytes 294920 | tf_op jit(solution)/shard_map/ppermute | solution.py:94
  39.8 6.8 %collective-permute-start.8 = (bf16[128,384]{1,0:T(8,128)(2,1)S(1)}, bf16[128,384]{1,0:T(8,128)(2,1)S(1)}, u32[]{:S(2)}, u32[]{:S(2)}) collective-permute-start(bf16[128,384]{1,0:T(8,128)(2,1)S(1)} %collective-permute-done.6), channel_id=1, source_target_pairs={{0,1},{1,2},{2,3},{3,4},{4,5},{5,6},{6,7},{7,8},{8,9},{9,10},{10,1... | collective-permute-start | bytes 294920 | tf_op jit(solution)/shard_map/ppermute | solution.py:89
  39.8 6.8 %collective-permute-start.9 = (bf16[128,384]{1,0:T(8,128)(2,1)S(1)}, bf16[128,384]{1,0:T(8,128)(2,1)S(1)}, u32[]{:S(2)}, u32[]{:S(2)}) collective-permute-start(bf16[128,384]{1,0:T(8,128)(2,1)S(1)} %collective-permute-done.7), channel_id=1, source_target_pairs={{0,15},{1,0},{2,1},{3,2},{4,3},{5,4},{6,5},{7,6},{8,7},{9,8},{10,9... | collective-permute-start | bytes 294920 | tf_op jit(solution)/shard_map/ppermute | solution.py:94
  46.6 6.7 %collective-permute-start.10 = (bf16[128,384]{1,0:T(8,128)(2,1)S(1)}, bf16[128,384]{1,0:T(8,128)(2,1)S(1)}, u32[]{:S(2)}, u32[]{:S(2)}) collective-permute-start(bf16[128,384]{1,0:T(8,128)(2,1)S(1)} %collective-permute-done.8), channel_id=1, source_target_pairs={{0,1},{1,2},{2,3},{3,4},{4,5},{5,6},{6,7},{7,8},{8,9},{9,10},{10,1... | collective-permute-start | bytes 294920 | tf_op jit(solution)/shard_map/ppermute | solution.py:89
  46.7 6.7 %collective-permute-start.11 = (bf16[128,384]{1,0:T(8,128)(2,1)S(1)}, bf16[128,384]{1,0:T(8,128)(2,1)S(1)}, u32[]{:S(2)}, u32[]{:S(2)}) collective-permute-start(bf16[128,384]{1,0:T(8,128)(2,1)S(1)} %collective-permute-done.9), channel_id=1, source_target_pairs={{0,15},{1,0},{2,1},{3,2},{4,3},{5,4},{6,5},{7,6},{8,7},{9,8},{10,9... | collective-permute-start | bytes 294920 | tf_op jit(solution)/shard_map/ppermute | solution.py:94
  53.4 6.7 %collective-permute-start.12 = (bf16[128,384]{1,0:T(8,128)(2,1)S(1)}, bf16[128,384]{1,0:T(8,128)(2,1)S(1)}, u32[]{:S(2)}, u32[]{:S(2)}) collective-permute-start(bf16[128,384]{1,0:T(8,128)(2,1)S(1)} %collective-permute-done.10), channel_id=1, source_target_pairs={{0,1},{1,2},{2,3},{3,4},{4,5},{5,6},{6,7},{7,8},{8,9},{9,10},{10,1... | collective-permute-start | bytes 294920 | tf_op jit(solution)/shard_map/ppermute | solution.py:89
  53.4 6.8 %collective-permute-start.13 = (bf16[128,384]{1,0:T(8,128)(2,1)S(1)}, bf16[128,384]{1,0:T(8,128)(2,1)S(1)}, u32[]{:S(2)}, u32[]{:S(2)}) collective-permute-start(bf16[128,384]{1,0:T(8,128)(2,1)S(1)} %collective-permute-done.11), channel_id=1, source_target_pairs={{0,15},{1,0},{2,1},{3,2},{4,3},{5,4},{6,5},{7,6},{8,7},{9,8},{10,9... | collective-permute-start | bytes 294920 | tf_op jit(solution)/shard_map/ppermute | solution.py:94
  60.1 6.8 %collective-permute-start.14 = (bf16[128,384]{1,0:T(8,128)(2,1)S(1)}, bf16[128,384]{1,0:T(8,128)(2,1)S(1)}, u32[]{:S(2)}, u32[]{:S(2)}) collective-permute-start(bf16[128,384]{1,0:T(8,128)(2,1)S(1)} %collective-permute-done.12), channel_id=1, source_target_pairs={{0,1},{1,2},{2,3},{3,4},{4,5},{5,6},{6,7},{7,8},{8,9},{9,10},{10,1... | collective-permute-start | bytes 294920 | tf_op jit(solution)/shard_map/ppermute | solution.py:89
  60.2 6.8 %collective-permute-start.15 = (bf16[128,384]{1,0:T(8,128)(2,1)S(1)}, bf16[128,384]{1,0:T(8,128)(2,1)S(1)}, u32[]{:S(2)}, u32[]{:S(2)}) collective-permute-start(bf16[128,384]{1,0:T(8,128)(2,1)S(1)} %collective-permute-done.13), channel_id=1, source_target_pairs={{0,15},{1,0},{2,1},{3,2},{4,3},{5,4},{6,5},{7,6},{8,7},{9,8},{10,9... | collective-permute-start | bytes 294920 | tf_op jit(solution)/shard_map/ppermute | solution.py:94
  66.9 6.7 %collective-permute-start.16 = (bf16[128,384]{1,0:T(8,128)(2,1)S(1)}, bf16[128,384]{1,0:T(8,128)(2,1)S(1)}, u32[]{:S(2)}, u32[]{:S(2)}) collective-permute-start(bf16[128,384]{1,0:T(8,128)(2,1)S(1)} %collective-permute-done.14), channel_id=1, source_target_pairs={{0,1},{1,2},{2,3},{3,4},{4,5},{5,6},{6,7},{7,8},{8,9},{9,10},{10,1... | collective-permute-start | bytes 294920 | tf_op jit(solution)/shard_map/ppermute | solution.py:89
  67.0 6.8 %collective-permute-start.17 = (bf16[128,384]{1,0:T(8,128)(2,1)S(1)}, bf16[128,384]{1,0:T(8,128)(2,1)S(1)}, u32[]{:S(2)}, u32[]{:S(2)}) collective-permute-start(bf16[128,384]{1,0:T(8,128)(2,1)S(1)} %collective-permute-done.15), channel_id=1, source_target_pairs={{0,15},{1,0},{2,1},{3,2},{4,3},{5,4},{6,5},{7,6},{8,7},{9,8},{10,9... | collective-permute-start | bytes 294920 | tf_op jit(solution)/shard_map/ppermute | solution.py:94
  73.6 6.7 %collective-permute-start.18 = (bf16[128,384]{1,0:T(8,128)(2,1)S(1)}, bf16[128,384]{1,0:T(8,128)(2,1)S(1)}, u32[]{:S(2)}, u32[]{:S(2)}) collective-permute-start(bf16[128,384]{1,0:T(8,128)(2,1)S(1)} %collective-permute-done.16), channel_id=1, source_target_pairs={{0,1},{1,2},{2,3},{3,4},{4,5},{5,6},{6,7},{7,8},{8,9},{9,10},{10,1... | collective-permute-start | bytes 294920 | tf_op jit(solution)/shard_map/ppermute | solution.py:89
  80.4 1.9 %copy-start.9 = (f32[384]{0:T(512)S(1)}, f32[384]{0:T(512)}, u32[]{:S(2)}) copy-start(f32[384]{0:T(512)} %param.25) | copy-start | bytes 4612
  82.3 2.6 %copy-start.3 = (bf16[384,384]{1,0:T(8,128)(2,1)S(1)}, bf16[384,384]{1,0:T(8,128)(2,1)}, u32[]{:S(2)}) copy-start(bf16[384,384]{1,0:T(8,128)(2,1)} %param.26) | copy-start | bytes 884740
  82.3 2.6 %copy-start.8 = (f32[384]{0:T(512)S(1)}, f32[384]{0:T(512)}, u32[]{:S(2)}) copy-start(f32[384]{0:T(512)} %param.27) | copy-start | bytes 4612
